TPU v7x, 32 devices: a whole 2x2x4 slice. The times are simulated.
32 devices in a mesh: fsdp: 8 (over z, x), rep: 4 (over y, core).
Axes of the slice: x: 2, y: 2, z: 4, core: 2. Of those that a mesh axis runs over, the one named last changes fastest.
Arguments:
- tokens_x: bfloat16 [4096, 8192], P(('fsdp', 'rep')), may hold values from -6 to 6
- cotangent: bfloat16 [4096, 128], P(('fsdp', 'rep')), may hold values from -1 to 1
- master_weight: float32 [8192, 128], P('fsdp'), may hold values from -0.015625 to 0.015625
- first_moment: float32 [8192, 128], P('fsdp'), may hold values from -6 to 6
- second_moment: float32 [8192, 128], P('fsdp'), may hold values from 0.5 to 2
- hidden_dec: bfloat16 [2, 64, 8192], P(None, ('fsdp', 'rep')), may hold values from -6 to 6
- queries: bfloat16 [2, 64, 1024], P(None, ('fsdp', 'rep')), may hold values from -64 to 64
- new_values: bfloat16 [2, 64, 128], P(None, ('fsdp', 'rep')), may hold values from -6 to 6
- key_cache: bfloat16 [64, 1024, 128], P(('fsdp', 'rep')), may hold values from -64 to 64
- value_cache: bfloat16 [64, 1024, 128], P(('fsdp', 'rep')), may hold values from -6 to 6
- cache_lengths: int32 [64], P(('fsdp', 'rep')), may hold values from 2 to 1022, as said below
Outputs:
- weight_next: float32 [8192, 128], P('fsdp')
- first_next: float32 [8192, 128], P('fsdp')
- second_next: float32 [8192, 128], P('fsdp')
- rollout_weight: bfloat16 [8192, 128], replicated
- fresh_keys: bfloat16 [2, 64, 128], P(None, ('fsdp', 'rep'))
- attended: bfloat16 [2, 64, 1024], P(None, ('fsdp', 'rep'))
Inputs may be any that keep to these rules, and one draw needn't show every extreme that they name: `cache_lengths`: some row has exactly 1022 filled slots.
All inputs are finite; a program needn't handle non-finite values. Where the computation divides by a largest or mean magnitude, that divisor is 1e-20 or more.
Results may differ from a plain program's by a relative error of at most 0.0049.
Values may be sent and summed in bfloat16 or wider, within the bound.
A program may use at most 64 MiB of HBM per device.

v0:
```python
import math
import jax
import jax.numpy as jnp
from jax import lax
from jax.sharding import PartitionSpec as P

D = 8192
BLOCK = 128
beta_one = 0.9
beta_two = 0.95
adam_eps = 1e-08
learn_rate = 0.0003
weight_decay = 0.1
step_count = 100
rope_theta = 1000000.0
peak_eps = 1e-06


def adamw(weight, first, second, gradient):
    first_new = beta_one * first + (1.0 - beta_one) * gradient
    second_new = beta_two * second + (1.0 - beta_two) * gradient * gradient
    first_hat = first_new / (1.0 - beta_one**step_count)
    second_hat = second_new / (1.0 - beta_two**step_count)
    weight_new = weight - learn_rate * (
        first_hat / (jnp.sqrt(second_hat) + adam_eps) + weight_decay * weight
    )
    return (weight_new, first_new, second_new)


def rotate(values, positions):
    half = values.shape[-1] // 2
    freq = rope_theta ** (-jnp.arange(half, dtype=jnp.float32) * 2.0 / values.shape[-1])
    angle = positions.astype(jnp.float32)[..., None] * freq
    cosine = jnp.cos(angle)
    sine = jnp.sin(angle)
    first_half = values[..., :half]
    second_half = values[..., half:]
    return jnp.concatenate(
        [first_half * cosine - second_half * sine, second_half * cosine + first_half * sine],
        axis=-1,
    )


def project_keys(hidden_size, quantized_weight, scales, lengths):
    decode_step_count, row_count, block_width = hidden_size.shape
    block_count = scales.shape[0]
    part_count = jnp.einsum(
        "qht,hti->qhi",
        hidden_size.reshape(decode_step_count * row_count, block_count, block_width // block_count),
        quantized_weight.reshape(block_count, block_width // block_count, -1),
        preferred_element_type=jnp.float32,
    )
    raw = jnp.sum(part_count * scales[None, :, None], axis=1).reshape(
        decode_step_count, row_count, -1
    )
    positions = lengths[None, :] + jnp.arange(decode_step_count, dtype=jnp.int32)[:, None]
    return rotate(raw, positions).astype(jnp.bfloat16)


def attend(query, cache_keys, cache_values, fresh, fresh_values, lengths):
    decode_step_count, row_count, joined = query.shape
    head_dim = cache_keys.shape[-1]
    heads = joined // head_dim
    valid = jnp.arange(cache_keys.shape[1], dtype=jnp.int32)[None, None, :] < lengths[:, None, None]
    outputs = []
    for section_index in range(decode_step_count):
        query_now = query[section_index].reshape(row_count, heads, head_dim)
        scores_c = jnp.einsum(
            "rhd,rcd->rhc", query_now, cache_keys, preferred_element_type=jnp.float32
        ) / math.sqrt(head_dim)
        scores_f = jnp.einsum(
            "rhd,trd->rht", query_now, fresh, preferred_element_type=jnp.float32
        ) / math.sqrt(head_dim)
        scores_c = jnp.where(valid, scores_c, -jnp.inf)
        scores_f = jnp.where(
            (jnp.arange(decode_step_count) <= section_index)[None, None, :], scores_f, -jnp.inf
        )
        peak = jnp.maximum(jnp.max(scores_c, axis=2), jnp.max(scores_f, axis=2))[:, :, None]
        exp_c = jnp.exp(scores_c - peak)
        exp_f = jnp.exp(scores_f - peak)
        total = jnp.sum(exp_c, axis=2, keepdims=True) + jnp.sum(exp_f, axis=2, keepdims=True)
        prob_c = (exp_c / total).astype(jnp.bfloat16)
        prob_f = (exp_f / total).astype(jnp.bfloat16)
        mixed = jnp.einsum("rhc,rcd->rhd", prob_c, cache_values, preferred_element_type=jnp.float32)
        mixed = mixed + jnp.einsum(
            "rht,trd->rhd", prob_f, fresh_values, preferred_element_type=jnp.float32
        )
        outputs.append(mixed.reshape(row_count, joined).astype(jnp.bfloat16))
    return jnp.stack(outputs)


def shards(
    tokens_x,
    cotangent,
    master_weight,
    first_moment,
    second_moment,
    hidden_dec,
    queries,
    new_values,
    key_cache,
    value_cache,
    cache_lengths,
):
    shard_rows = master_weight.shape[0]
    partial_grad = lax.psum_scatter(
        lax.dot_general(
            tokens_x, cotangent, (((0,), (0,)), ((), ())), preferred_element_type=jnp.float32
        ),
        "fsdp",
        scatter_dimension=0,
        tiled=True,
    )
    gradient = lax.psum(partial_grad, "rep")
    weight_next, first_next, second_next = adamw(
        master_weight, first_moment, second_moment, gradient
    )
    block_count = D // BLOCK
    row_ids = lax.axis_index("fsdp") * shard_rows + jnp.arange(shard_rows, dtype=jnp.int32)
    member = (row_ids // BLOCK)[:, None] == jnp.arange(block_count, dtype=jnp.int32)[None, :]
    row_peak = jnp.max(jnp.abs(weight_next), axis=1)
    local_peaks = jnp.max(jnp.where(member, row_peak[:, None], 0.0), axis=0)
    scales = lax.pmax(local_peaks, "fsdp") + peak_eps
    row_scale = jnp.sum(jnp.where(member, scales[None, :], 0.0), axis=1)
    local_quant = (weight_next / row_scale[:, None]).astype(jnp.bfloat16)
    rollout_weight = lax.all_gather(local_quant, "fsdp", axis=0, tiled=True)
    fresh_keys = project_keys(hidden_dec, rollout_weight, scales, cache_lengths)
    attended = attend(queries, key_cache, value_cache, fresh_keys, new_values, cache_lengths)
    return (weight_next, first_next, second_next, rollout_weight, fresh_keys, attended)


def solution(mesh):
    return jax.shard_map(
        shards,
        mesh=mesh,
        in_specs=(
            P(("fsdp", "rep"), None),
            P(("fsdp", "rep"), None),
            P("fsdp", None),
            P("fsdp", None),
            P("fsdp", None),
            P(None, ("fsdp", "rep"), None),
            P(None, ("fsdp", "rep"), None),
            P(None, ("fsdp", "rep"), None),
            P(("fsdp", "rep"), None, None),
            P(("fsdp", "rep"), None, None),
            P(("fsdp", "rep")),
        ),
        out_specs=(
            P("fsdp", None),
            P("fsdp", None),
            P("fsdp", None),
            P(),
            P(None, ("fsdp", "rep"), None),
            P(None, ("fsdp", "rep"), None),
        ),
        check_vma=False,
    )
```

profile of v0, /device:TPU:0, one launch (start us, length us, event | category | flops | bytes accessed | tf_op | source)
XLA Modules:
  0.0 224.9 jit_solution(2394929650028422589)
XLA Ops:
  7.2 1.5 copy-done
  8.8 3.4 %fusion.52 = f32[8192,128]{1,0:T(8,128)} fusion(bf16[128,8192]{1,0:T(8,128)(2,1)S(1)} %copy-done, bf16[128,128]{1,0:T(8,128)(2,1)} %param.12), kind=kOutput, calls=%fused_computation.92 | convolution fusion | flops 268435456 | bytes 6324224 | tf_op jit(solution)/shard_map/dot_general | solution.py:107
  12.3 91.1 %reduce-scatter.2.cloned.1.call-done = f32[1024,128]{1,0:T(8,128)} async-done(((f32[8192,128]{1,0:T(8,128)}), f32[1024,128]{1,0:T(8,128)}) %reduce-scatter.2.cloned.1.call-update) | async-done | bytes 524304 | tf_op jit(solution)/shard_map/reduce_scatter | solution.py:106
  103.6 35.3 %all-reduce.2.cloned.1.call-done = f32[1024,128]{1,0:T(8,128)} async-done(((f32[1024,128]{1,0:T(8,128)}), f32[1024,128]{1,0:T(8,128)}) %all-reduce.2.cloned.1.call-update) | async-done | bytes 524304 | tf_op jit(solution)/shard_map/psum | solution.py:114
  138.8 2.9 %abs_reduce_fusion = (f32[1024]{0:T(1024)S(1)}, f32[1024,128]{1,0:T(8,128)S(1)}, f32[1024,128]{1,0:T(8,128)}, f32[1024,128]{1,0:T(8,128)}) fusion(f32[1024,128]{1,0:T(8,128)} %param.13, f32[1024,128]{1,0:T(8,128)} %all-reduce.2.cloned.1.call-done, f32[1024,128]{1,0:T(8,128)} %param.14, f32[1024,128]{1,0:T(8,128)} %param.15), kind=kLoop, calls=%fused_computation.19 | loop fusion | flops 2227200 | bytes 3674112 | tf_op jit(solution)/shard_map/reduce_max | solution.py:121
  141.7 0.1 select_reduce_fusion.1
  141.9 21.3 %pmax.7 = f32[64]{0:T(128)S(1)} all-reduce(f32[64]{0:T(128)S(1)} %select_reduce_fusion.1), channel_id=1, replica_groups=mesh['fsdp'=8,'rep'=4] {'fsdp'}, use_global_device_ids=true, to_apply=%region_4.5 | all-reduce | flops 64 | bytes 512 | tf_op jit(solution)/shard_map/pmax | solution.py:123
  163.3 0.9 divide_convert_fusion
  164.6 0.3 fusion.50
  164.9 0.3 fusion.48
  165.3 44.7 %all-gather.2.cloned.1.call-done = bf16[8192,128]{1,0:T(8,128)(2,1)} async-done(((bf16[1024,128]{1,0:T(8,128)(2,1)}), bf16[8192,128]{1,0:T(8,128)(2,1)}) %all-gather.2.cloned.1.call-update) | async-done | bytes 2097168 | tf_op jit(solution)/shard_map/all_gather | solution.py:126
  210.0 2.2 fusion
  212.3 0.1 fusion.37
  212.5 0.6 copy.32
  213.1 0.1 fusion.49
  213.2 0.1 fusion.51
  213.4 0.2 fusion.12
  213.5 0.2 fusion.14
  213.8 0.2 fusion.4
  214.0 0.2 fusion.11
  214.2 0.2 fusion.13
  214.5 0.2 fusion.3
  214.7 0.6 pad_maximum_fusion
  215.3 3.0 %copy.73 = bf16[8192,128]{1,0:T(8,128)(2,1)} copy(bf16[8192,128]{1,0:T(8,128)(2,1)} %all-gather.2.cloned.1.call-done) | data formatting | bytes 4194304
  (41 shorter events, 0.8 us)
Async XLA Ops:
  7.2 1.6 copy-start
  7.2 96.2 %reduce-scatter.2.cloned.1.call-start = ((), (), s32[]{:S(2)}) async-start(), calls=%async_computation.1 | async-start | bytes 4718592 | tf_op jit(solution)/shard_map/reduce_scatter | solution.py:106
  12.2 126.6 %all-reduce.2.cloned.1.call-start = ((), (), s32[]{:S(2)}) async-start(), calls=%async_computation.2 | async-start | bytes 1048576 | tf_op jit(solution)/shard_map/psum | solution.py:114
  103.4 106.5 %all-gather.2.cloned.1.call-start = ((), (), s32[]{:S(2)}) async-start(), calls=%async_computation.3 | async-start | bytes 2359296 | tf_op jit(solution)/shard_map/all_gather | solution.py:126
  103.5 60.8 %copy-start.4 = (bf16[2,2,8192]{2,1,0:T(2,128)(2,1)S(1)}, bf16[2,2,8192]{2,1,0:T(2,128)(2,1)}, u32[]{:S(2)}) copy-start(bf16[2,2,8192]{2,1,0:T(2,128)(2,1)} %param.16) | copy-start | bytes 196612
  103.5 60.9 %copy-start.6 = (s32[2]{0:T(128)S(1)}, s32[2]{0:T(128)}, u32[]{:S(2)}) copy-start(s32[2]{0:T(128)} %param.21) | copy-start | bytes 28
  103.5 61.0 %copy-start.5 = (bf16[2,2,1024]{2,1,0:T(2,128)(2,1)S(1)}, bf16[2,2,1024]{2,1,0:T(2,128)(2,1)}, u32[]{:S(2)}) copy-start(bf16[2,2,1024]{2,1,0:T(2,128)(2,1)} %param.17) | copy-start | bytes 24580
  103.5 61.0 %copy-start.1 = (bf16[2,1024,128]{2,1,0:T(8,128)(2,1)S(1)}, bf16[2,1024,128]{2,1,0:T(8,128)(2,1)}, u32[]{:S(2)}) copy-start(bf16[2,1024,128]{2,1,0:T(8,128)(2,1)} %param.19) | copy-start | bytes 1572868
  141.7 21.6 %copy-start.3 = (f32[1024,128]{1,0:T(8,128)}, f32[1024,128]{1,0:T(8,128)S(1)}, u32[]{:S(2)}) copy-start(f32[1024,128]{1,0:T(8,128)S(1)} %get-tuple-element.48) | copy-start | bytes 1572868
  164.3 49.3 %copy-start.2 = (bf16[2,1024,128]{2,1,0:T(8,128)(2,1)S(1)}, bf16[2,1024,128]{2,1,0:T(8,128)(2,1)}, u32[]{:S(2)}) copy-start(bf16[2,1024,128]{2,1,0:T(8,128)(2,1)} %param.20) | copy-start | bytes 1572868
  164.6 49.2 %copy-start.7 = (bf16[2,2,128]{2,1,0:T(2,128)(2,1)S(1)}, bf16[2,2,128]{2,1,0:T(2,128)(2,1)}, u32[]{:S(2)}) copy-start(bf16[2,2,128]{2,1,0:T(2,128)(2,1)} %param.18) | copy-start | bytes 3076
Sparse Core Ops, SparseCore 0:
  12.3 91.0 reduce-scatter.1
  105.8 33.0 all-reduce.1
  164.4 45.5 all-gather.1
where the time goes:
time: 225 us
  waiting for transfers between devices  171 us (76%)
  blocking collectives  21.3 us (9%)
  between operations  13.9 us (6%)
  matrix products  7.48 us (3%)
  other arithmetic  5.48 us (2%)
  local copies, waits for them, and re-layouts  5.36 us (2%)
    reduce_scatter x1, waiting for transfers between devices, shards(): lax.psum_scatter(lax.dot_general(tokens_x, cotangent, (((0,), (0,)), ((),...  91.1 us
    all_gather x1, waiting for transfers between devices, shards(): rollout_weight = lax.all_gather(local_quant, 'fsdp', axis=0, tiled=True)  44.7 us
    psum x1, waiting for transfers between devices, shards(): gradient = lax.psum(partial_grad, 'rep')  35.3 us
    pmax x1, blocking collectives, shards(): scales = lax.pmax(local_peaks, 'fsdp') + peak_eps  21.3 us
    unnamed x19, local copies, waits for them, and re-layouts  5.2 us
  transfers between devices with their start and end apart: 3, of which 3 were waited for; matrix products, arithmetic and copies ran while one was open for 0% of the time, Pallas kernels for 0%

commit v1 on v0

--- a/solution.py
+++ b/solution.py
@@ -111,7 +111,9 @@
         scatter_dimension=0,
         tiled=True,
     )
-    gradient = lax.psum(partial_grad, "rep")
+    gradient = partial_grad
+    for hop in (1, 2):
+        gradient = gradient + lax.ppermute(gradient, "rep", [(dev, dev ^ hop) for dev in range(4)])
     weight_next, first_next, second_next = adamw(
         master_weight, first_moment, second_moment, gradient
     )

time: 225 us -> 207 us (0.920)
  waiting for transfers between devices: 171 us -> 149 us
    psum x1 -> x0, waiting for transfers between devices: 35.3 us -> none  [shards(): gradient = lax.psum(partial_grad, 'rep')]
    ppermute x0 -> x2, waiting for transfers between devices: none -> 14.7 us  [shards(): lax.ppermute(gradient, 'rep', [(dev, dev ^ hop) for dev in range(4)])]
    unnamed x19 -> x17, local copies, waits for them, and re-layouts: 5.2 us -> 5.2 us
  transfers between devices with their start and end apart: 3 -> 4, of which waited for: 3 -> 4; matrix products, arithmetic and copies ran while one was open for 0% -> 1% of each run, Pallas kernels for 0% -> 0%
where the time goes in v1:
time: 207 us
  waiting for transfers between devices  149 us (72%)
  blocking collectives  20 us (10%)
  between operations  14.2 us (7%)
  matrix products  9.57 us (5%)
  other arithmetic  6.62 us (3%)
  local copies, waits for them, and re-layouts  5.36 us (3%)
    reduce_scatter x1, waiting for transfers between devices, shards(): lax.psum_scatter(lax.dot_general(tokens_x, cotangent, (((0,), (0,)), ((),...  91.1 us
    all_gather x1, waiting for transfers between devices, shards(): rollout_weight = lax.all_gather(local_quant, 'fsdp', axis=0, tiled=True)  43.5 us
    pmax x1, blocking collectives, shards(): scales = lax.pmax(local_peaks, 'fsdp') + peak_eps  20 us
    ppermute x2, waiting for transfers between devices, shards(): lax.ppermute(gradient, 'rep', [(dev, dev ^ hop) for dev in range(4)])  14.7 us
    unnamed x17, local copies, waits for them, and re-layouts  5.2 us
  transfers between devices with their start and end apart: 4, of which 4 were waited for; matrix products, arithmetic and copies ran while one was open for 1% of the time, Pallas kernels for 0%

profile of v1, /device:TPU:0, one launch (start us, length us, event | category | flops | bytes accessed | tf_op | source)
XLA Modules:
  0.0 206.7 jit_solution(8100989633884629714)
XLA Ops:
  7.2 1.5 copy-done
  8.8 3.4 %fusion.52 = f32[8192,128]{1,0:T(8,128)} fusion(bf16[128,8192]{1,0:T(8,128)(2,1)S(1)} %copy-done, bf16[128,128]{1,0:T(8,128)(2,1)} %param.12), kind=kOutput, calls=%fused_computation.92 | convolution fusion | flops 268435456 | bytes 6324224 | tf_op jit(solution)/shard_map/dot_general | solution.py:107
  12.3 91.1 %reduce-scatter.2.cloned.1.call-done = f32[1024,128]{1,0:T(8,128)} async-done(((f32[8192,128]{1,0:T(8,128)}), f32[1024,128]{1,0:T(8,128)}) %reduce-scatter.2.cloned.1.call-update) | async-done | bytes 524304 | tf_op jit(solution)/shard_map/reduce_scatter | solution.py:106
  103.4 2.1 %collective-permute-done = f32[1024,128]{1,0:T(8,128)S(1)} collective-permute-done((f32[1024,128]{1,0:T(8,128)}, f32[1024,128]{1,0:T(8,128)S(1)}, u32[]{:S(2)}, u32[]{:S(2)}) %collective-permute-start) | collective-permute-done | bytes 524320 | tf_op jit(solution)/shard_map/ppermute | solution.py:116
  105.5 1.1 add.86
  106.7 1.5 collective-permute-start.1
  108.2 12.6 %collective-permute-done.1 = f32[1024,128]{1,0:T(8,128)} collective-permute-done((f32[1024,128]{1,0:T(8,128)S(1)}, f32[1024,128]{1,0:T(8,128)}, u32[]{:S(2)}, u32[]{:S(2)}) %collective-permute-start.1) | collective-permute-done | bytes 524320 | tf_op jit(solution)/shard_map/ppermute | solution.py:116
  120.8 2.9 %abs_reduce_fusion = (f32[1024]{0:T(1024)S(1)}, f32[1024,128]{1,0:T(8,128)S(1)}, f32[1024,128]{1,0:T(8,128)}, f32[1024,128]{1,0:T(8,128)}) fusion(f32[1024,128]{1,0:T(8,128)} %param.13, f32[1024,128]{1,0:T(8,128)S(1)} %add.86, f32[1024,128]{1,0:T(8,128)} %collective-permute-done.1, f32[1024,128]{1,0:T(8,128)} %param.14, f32[1024,128]{1,0:T(8,128)} %param.15), kind=kLoop, calls=%fused_computation.19 | loop fusion | flops 2358272 | bytes 4198400 | tf_op jit(solution)/shard_map/reduce_max | solution.py:123
  123.8 20.0 %pmax.7 = f32[64]{0:T(128)S(1)} all-reduce(f32[64]{0:T(128)S(1)} %select_reduce_fusion.1), channel_id=1, replica_groups=mesh['fsdp'=8,'rep'=4] {'fsdp'}, use_global_device_ids=true, to_apply=%region_3.4 | all-reduce | flops 64 | bytes 512 | tf_op jit(solution)/shard_map/pmax | solution.py:125
  144.0 0.9 divide_convert_fusion
  145.2 1.4 fusion.50
  146.6 1.4 fusion.48
  148.0 43.5 %all-gather.2.cloned.1.call-done = bf16[8192,128]{1,0:T(8,128)(2,1)} async-done(((bf16[1024,128]{1,0:T(8,128)(2,1)}), bf16[8192,128]{1,0:T(8,128)(2,1)}) %all-gather.2.cloned.1.call-update) | async-done | bytes 2097168 | tf_op jit(solution)/shard_map/all_gather | solution.py:128
  191.4 2.2 %fusion = f32[128,4]{0,1:T(4,128)S(1)} fusion(bf16[64,128,128]{2,1,0:T(8,128)(2,1)} %bitcast.41, bf16[4,64,128]{2,1,0:T(8,128)(2,1)S(1)} %reshape.145, f32[64]{0:T(128)S(1)} %broadcast_add_fusion), kind=kOutput, calls=%fused_computation.1 | convolution fusion | flops 8453632 | bytes 2164992 | tf_op jit(solution)/shard_map/qht,hti->qhi/dot_general | solution.py:47
  194.0 0.6 copy.32
  194.5 0.1 fusion.49
  194.8 0.2 fusion.12
  195.0 0.2 fusion.14
  195.3 0.2 fusion.4
  195.5 0.2 fusion.11
  195.7 0.2 fusion.13
  195.9 0.2 fusion.3
  196.2 0.6 pad_maximum_fusion
  196.8 3.0 %copy.72 = bf16[8192,128]{1,0:T(8,128)(2,1)} copy(bf16[8192,128]{1,0:T(8,128)(2,1)} %all-gather.2.cloned.1.call-done) | data formatting | bytes 4194304
  (41 shorter events, 1.2 us)
Async XLA Ops:
  7.2 1.6 copy-start
  7.2 96.2 %reduce-scatter.2.cloned.1.call-start = ((), (), s32[]{:S(2)}) async-start(), calls=%async_computation.1 | async-start | bytes 4718592 | tf_op jit(solution)/shard_map/reduce_scatter | solution.py:106
  12.2 179.2 %all-gather.2.cloned.1.call-start = ((), (), s32[]{:S(2)}) async-start(), calls=%async_computation.2 | async-start | bytes 2359296 | tf_op jit(solution)/shard_map/all_gather | solution.py:128
  103.4 2.1 %collective-permute-start = (f32[1024,128]{1,0:T(8,128)}, f32[1024,128]{1,0:T(8,128)S(1)}, u32[]{:S(2)}, u32[]{:S(2)}) collective-permute-start(f32[1024,128]{1,0:T(8,128)} %reduce-scatter.2.cloned.1.call-done), channel_id=1, source_target_pairs={{0,1},{1,0},{2,3},{3,2},{4,5},{5,4},{6,7},{7,6},{8,9},{9,8},{10,11... | collective-permute-start | bytes 1572872 | tf_op jit(solution)/shard_map/ppermute | solution.py:116
  106.7 14.1 %collective-permute-start.1 = (f32[1024,128]{1,0:T(8,128)S(1)}, f32[1024,128]{1,0:T(8,128)}, u32[]{:S(2)}, u32[]{:S(2)}) collective-permute-start(f32[1024,128]{1,0:T(8,128)S(1)} %add.86), channel_id=1, source_target_pairs={{0,2},{1,3},{2,0},{3,1},{4,6},{5,7},{6,4},{7,5},{8,10},{9,11},{10,... | collective-permute-start | bytes 1572872 | tf_op jit(solution)/shard_map/ppermute | solution.py:116
  108.2 36.7 %copy-start.3 = (bf16[2,2,8192]{2,1,0:T(2,128)(2,1)S(1)}, bf16[2,2,8192]{2,1,0:T(2,128)(2,1)}, u32[]{:S(2)}) copy-start(bf16[2,2,8192]{2,1,0:T(2,128)(2,1)} %param.16) | copy-start | bytes 196612
  108.2 36.8 %copy-start.5 = (s32[2]{0:T(128)S(1)}, s32[2]{0:T(128)}, u32[]{:S(2)}) copy-start(s32[2]{0:T(128)} %param.21) | copy-start | bytes 28
  108.2 37.0 %copy-start.4 = (bf16[2,2,1024]{2,1,0:T(2,128)(2,1)S(1)}, bf16[2,2,1024]{2,1,0:T(2,128)(2,1)}, u32[]{:S(2)}) copy-start(bf16[2,2,1024]{2,1,0:T(2,128)(2,1)} %param.17) | copy-start | bytes 24580
  123.7 70.0 %copy-start.1 = (f32[1024,128]{1,0:T(8,128)}, f32[1024,128]{1,0:T(8,128)S(1)}, u32[]{:S(2)}) copy-start(f32[1024,128]{1,0:T(8,128)S(1)} %get-tuple-element.48) | copy-start | bytes 1572868
  144.9 50.1 %copy-start.2 = (bf16[2,1024,128]{2,1,0:T(8,128)(2,1)S(1)}, bf16[2,1024,128]{2,1,0:T(8,128)(2,1)}, u32[]{:S(2)}) copy-start(bf16[2,1024,128]{2,1,0:T(8,128)(2,1)} %param.20) | copy-start | bytes 1572868
  145.2 50.0 %copy-start.6 = (bf16[2,2,128]{2,1,0:T(2,128)(2,1)S(1)}, bf16[2,2,128]{2,1,0:T(2,128)(2,1)}, u32[]{:S(2)}) copy-start(bf16[2,2,128]{2,1,0:T(2,128)(2,1)} %param.18) | copy-start | bytes 3076
Sparse Core Ops, SparseCore 0:
  12.3 91.0 reduce-scatter.1
  145.1 46.3 all-gather.1
